TPU v7x, 32 devices: a whole 2x2x4 slice. The times are simulated.
32 devices in a mesh: str: 8 (over z, x), fac: 4 (over y, core).
Axes of the slice: x: 2, y: 2, z: 4, core: 2. Of those that a mesh axis runs over, the one named last changes fastest.
Arguments:
- amplitudes: bfloat16 [2, 4096, 4096], P(None, 'str'), may hold values from -6 to 6
- beta_index: int32 [2, 32, 12], replicated, may hold values from 0 to 31, all different within a row; in each aligned block of 32 rows (0 to 31, 32 to 63, ..., all dimensions but the last counted through in order) at most 24 rows name the same one
- beta_tile: int32 [2, 12], replicated, may hold values from 0 to 15
- beta_flip: int32 [2, 4096], replicated, may hold values 0 or 1
- alpha_index: int32 [2, 32, 12], replicated, may hold values from 0 to 31, all different within a row; in each aligned block of 32 rows (0 to 31, 32 to 63, ..., all dimensions but the last counted through in order) at most 24 rows name the same one
- alpha_tile: int32 [2, 12], replicated, may hold values from 0 to 15
- alpha_flip: int32 [2, 4096], replicated, may hold values 0 or 1
- beta_tiles: bfloat16 [16, 128, 128], replicated, may hold values from -0.15625 to 0.15625
- alpha_tiles: bfloat16 [16, 128, 128], replicated, may hold values from -0.109375 to 0.109375
Outputs:
- sigma: float32 [2, 4096, 4096], P(None, 'fac', 'str')
Inputs may be any that keep to these rules, and one draw needn't show every extreme that they name: `beta_index`: each block row of one factor's beta operator names 12 different block columns; within one factor's operator no block column is named by more than 24 block rows, and in some factor one column is named by exactly 24. `alpha_index`: each block row of one factor's alpha operator names 12 different block columns; within one factor's operator no block column is named by more than 24 block rows, and in some factor one column is named by exactly 24.
All inputs are finite; a program needn't handle non-finite values.
Results may differ from a plain program's by a relative error of at most 0.012.
Values may be sent and summed in bfloat16 or wider, within the bound.
A program may use at most 128 MiB of HBM per device.

v0:
```python
import jax
import jax.numpy as jnp
from jax import lax
from jax.sharding import PartitionSpec as P


def apply_beta(amplitudes, block_ids, tile_ids, flips, tile_table):
    part_count, height, column_count = amplitudes.shape
    tile_size = tile_table.shape[1]
    block_count = column_count // tile_size
    signs = (1 - 2 * flips).astype(jnp.bfloat16)
    signed = amplitudes * signs[None, None, :]
    blocks = signed.reshape(part_count, height, block_count, tile_size)
    weights = tile_table[tile_ids]
    group_size = block_count // 4
    pieces = []
    for group_id in range(4):
        lower = group_id * group_size
        chosen = block_ids[lower : lower + group_size]
        gathered = blocks[:, :, chosen]
        pieces.append(
            jnp.einsum(
                "pajkc,krc->pajr", gathered, weights, preferred_element_type=jnp.float32
            ).astype(jnp.bfloat16)
        )
    return jnp.concatenate(pieces, axis=2).reshape(part_count, height, column_count)


def apply_alpha(half, block_ids, tile_ids, flips, tile_table):
    part_count, total, column_count = half.shape
    tile_size = tile_table.shape[1]
    block_count = total // tile_size
    signs = (1 - 2 * flips).astype(jnp.bfloat16)
    signed = half * signs[None, :, None]
    blocks = signed.reshape(part_count, block_count, tile_size, column_count)
    weights = tile_table[tile_ids]
    group_size = block_count // 4
    pieces = []
    for group_id in range(4):
        lower = group_id * group_size
        chosen = block_ids[lower : lower + group_size]
        gathered = blocks[:, chosen]
        pieces.append(
            jnp.einsum(
                "pjkcn,krc->pjrn", gathered, weights, preferred_element_type=jnp.float32
            ).astype(jnp.bfloat16)
        )
    return jnp.concatenate(pieces, axis=1).reshape(part_count, total, column_count)


def local(
    amplitudes,
    beta_index,
    beta_tile,
    beta_flip,
    alpha_index,
    alpha_tile,
    alpha_flip,
    beta_tiles,
    alpha_tiles,
):
    position = lax.axis_index("fac")
    factor = position // 2
    part = position % 2
    own_part = lax.dynamic_index_in_dim(amplitudes, part, 0, keepdims=True)
    beta_ids = lax.dynamic_index_in_dim(beta_index, factor, 0, keepdims=False)
    beta_kinds = lax.dynamic_index_in_dim(beta_tile, factor, 0, keepdims=False)
    beta_signs = lax.dynamic_index_in_dim(beta_flip, factor, 0, keepdims=False)
    half = apply_beta(own_part, beta_ids, beta_kinds, beta_signs, beta_tiles)
    alpha_ids = lax.dynamic_index_in_dim(alpha_index, factor, 0, keepdims=False)
    alpha_kinds = lax.dynamic_index_in_dim(alpha_tile, factor, 0, keepdims=False)
    alpha_signs = lax.dynamic_index_in_dim(alpha_flip, factor, 0, keepdims=False)
    mixed = apply_alpha(
        lax.all_to_all(half, "str", split_axis=2, concat_axis=1, tiled=True),
        alpha_ids,
        alpha_kinds,
        alpha_signs,
        alpha_tiles,
    )
    mixed = lax.optimization_barrier(mixed)
    selector = (jnp.arange(2) == part)[:, None, None]
    padded = jnp.where(selector, mixed.astype(jnp.float32), 0.0)
    return lax.psum_scatter(
        padded.astype(jnp.bfloat16), "fac", scatter_dimension=1, tiled=True
    ).astype(jnp.float32)


def solution(mesh):
    return jax.shard_map(
        local,
        mesh=mesh,
        in_specs=(P(None, "str", None), P(), P(), P(), P(), P(), P(), P(), P()),
        out_specs=P(None, "fac", "str"),
        check_vma=False,
    )
```

profile of v0, /device:TPU:0, one launch (start us, length us, event | category | flops | bytes accessed | tf_op | source)
XLA Modules:
  0.0 445.0 jit_solution(6631989853623679221)
XLA Ops:
  6.5 0.0 copy-start
  6.5 4.8 %constant_dynamic-slice_fusion.9 = bf16[1,512,4096]{2,1,0:T(8,128)(2,1)} fusion(bf16[2,512,4096]{2,1,0:T(8,128)(2,1)} %param.9, s32[]{:T(128)S(6)} %select_n.134), kind=kLoop, calls=%fused_computation.69 | loop fusion | bytes 8388612 | tf_op jit(solution)/shard_map/jit(dynamic_index_in_dim)/dynamic_slice | solution.py:65
  11.3 6.5 %copy.44 = bf16[1,512,4096]{1,2,0:T(8,128)(2,1)} copy(bf16[1,512,4096]{2,1,0:T(8,128)(2,1)} %constant_dynamic-slice_fusion.9) | data formatting | bytes 8388608
  17.8 0.0 copy-done.10
  17.8 0.1 convert_reduce_fusion
  17.9 0.0 copy-start.12
  17.9 0.0 copy-start.13
  17.9 4.0 broadcast_multiply_fusion
  21.9 6.4 %copy.28 = bf16[512,32,128]{2,0,1:T(8,128)(2,1)} copy(bf16[512,32,128]{0,2,1:T(8,128)(2,1)} %bitcast.181) | data formatting | bytes 8388608 | tf_op jit(solution)/shard_map/reshape | solution.py:13
  28.3 0.1 constant_dynamic-slice_fusion.5
  28.4 0.1 copy.46
  28.5 0.1 copy.47
  28.6 0.1 reshape.415
  28.7 0.1 reshape.433
  28.8 9.0 %gather_fusion.1 = bf16[96,512,128]{2,1,0:T(8,128)(2,1)} fusion(bf16[512,32,128]{2,0,1:T(8,128)(2,1)} %copy.28, s32[1024]{0:T(1024)S(1)} %pad_clamp_fusion.8), kind=kCustom, calls=%fused_computation.1 | custom fusion | bytes 25166208 | tf_op jit(solution)/shard_map/gather | solution.py:20
  37.8 9.0 %gather_fusion.3 = bf16[96,512,128]{2,1,0:T(8,128)(2,1)} fusion(bf16[512,32,128]{2,0,1:T(8,128)(2,1)} %copy.28, s32[1024]{0:T(1024)S(1)} %pad_clamp_fusion.6), kind=kCustom, calls=%fused_computation.3 | custom fusion | bytes 25166208 | tf_op jit(solution)/shard_map/gather | solution.py:20
  46.8 0.6 gather_fusion.2
  47.5 8.9 %fusion = bf16[1,512,8,128]{1,3,2,0:T(8,128)(2,1)S(1)} fusion(bf16[512,8,12,128]{3,0,2,1:T(8,128)(2,1)} %bitcast.174, bf16[12,128,128]{2,1,0:T(8,128)(2,1)S(1)} %gather_fusion.2), kind=kOutput, calls=%fused_computation.24 | convolution fusion | flops 1611137024 | bytes 14024704 | tf_op jit(solution)/shard_map/pajkc,krc->pajr/dot_general | solution.py:22
  56.3 4.2 fusion.1
  60.5 0.1 copy.48
  60.6 0.1 copy.49
  60.7 0.1 reshape.443
  60.8 9.0 %gather_fusion.4 = bf16[96,512,128]{2,1,0:T(8,128)(2,1)} fusion(bf16[512,32,128]{2,0,1:T(8,128)(2,1)} %copy.28, s32[1024]{0:T(1024)S(1)} %pad_clamp_fusion.5), kind=kCustom, calls=%fused_computation.4 | custom fusion | bytes 25166208 | tf_op jit(solution)/shard_map/gather | solution.py:20
  69.8 9.7 %fusion.2 = bf16[1,512,8,128]{1,3,2,0:T(8,128)(2,1)} fusion(bf16[512,8,12,128]{3,0,2,1:T(8,128)(2,1)} %bitcast.177, bf16[12,128,128]{2,1,0:T(8,128)(2,1)S(1)} %gather_fusion.2), kind=kOutput, calls=%fused_computation.26 | convolution fusion | flops 1611137024 | bytes 14024704 | tf_op jit(solution)/shard_map/pajkc,krc->pajr/dot_general | solution.py:22
  79.5 0.1 reshape.453
  79.6 9.0 %gather_fusion.5 = bf16[96,512,128]{2,1,0:T(8,128)(2,1)} fusion(bf16[512,32,128]{2,0,1:T(8,128)(2,1)} %copy.28, s32[1024]{0:T(1024)S(1)} %pad_clamp_fusion.4), kind=kCustom, calls=%fused_computation.5 | custom fusion | bytes 25166208 | tf_op jit(solution)/shard_map/gather | solution.py:20
  88.6 8.8 %fusion.3 = bf16[1,512,8,128]{1,3,2,0:T(8,128)(2,1)S(1)} fusion(bf16[512,8,12,128]{3,0,2,1:T(8,128)(2,1)} %bitcast.176, bf16[12,128,128]{2,1,0:T(8,128)(2,1)S(1)} %gather_fusion.2), kind=kOutput, calls=%fused_computation.27 | convolution fusion | flops 1611137024 | bytes 14024704 | tf_op jit(solution)/shard_map/pajkc,krc->pajr/dot_general | solution.py:22
  97.5 0.6 pad_maximum_fusion
  98.0 36.5 %copy.56 = bf16[1,512,4096]{1,0,2:T(2,128)(2,1)} copy(bf16[1,512,4096]{1,2,0:T(8,128)(2,1)S(1)} %bitcast.178) | data formatting | bytes 8388608 | tf_op jit(solution)/shard_map/reshape | solution.py:26
  134.5 0.5 broadcast.272
  135.0 28.5 %reduce.4 = bf16[4096,512]{1,0:T(8,128)(2,1)} reduce(bf16[4096,1,512]{2,1,0:T(2,128)(2,1)} %bitcast.172, bf16[]{:T(256)} %broadcast.272), dimensions={1}, to_apply=%bitcast.167.reduce_sub_computation | reduce | bytes 8388610
  163.5 7.9 %reshape.535 = bf16[8,2,131072]{2,1,0:T(2,128)(2,1)} reshape(bf16[4096,512]{1,0:T(8,128)(2,1)} %reduce.4) | data formatting | bytes 8388608
  171.4 7.3 %all-to-all-start = ((bf16[8,2,131072]{2,1,0:T(2,128)(2,1)}), bf16[8,2,131072]{2,1,0:T(2,128)(2,1)}, u32[]{:S(2)}, u32[]{:S(2)}) async-start(bf16[8,2,131072]{2,1,0:T(2,128)(2,1)} %reshape.535), calls=%async_computation | async-start | bytes 8388608 | tf_op jit(solution)/shard_map/all_to_all | solution.py:74
  178.7 0.0 reduce-scatter.2.cloned.1.call-start
  178.8 0.1 constant_dynamic-slice_fusion.2
  178.9 0.1 copy.51
  179.0 0.1 copy.52
  179.1 0.1 reshape.463
  179.1 0.1 reshape.473
  179.2 0.1 copy.53
  179.3 0.1 copy.54
  179.4 0.1 reshape.483
  179.5 0.1 reshape.493
  179.6 0.6 gather_fusion
  180.3 91.7 %all-to-all-done = bf16[8,2,131072]{2,1,0:T(2,128)(2,1)} async-done(((bf16[8,2,131072]{2,1,0:T(2,128)(2,1)}), bf16[8,2,131072]{2,1,0:T(2,128)(2,1)}, u32[]{:S(2)}, u32[]{:S(2)}) %all-to-all-start) | async-done | bytes 4194336 | tf_op jit(solution)/shard_map/all_to_all | solution.py:74
  272.0 8.8 %reshape.536 = bf16[4096,1,512]{2,1,0:T(2,128)(2,1)} reshape(bf16[8,2,131072]{2,1,0:T(2,128)(2,1)} %all-to-all-done) | data formatting | bytes 8388608
  280.8 6.6 %copy.43 = bf16[1,512,4096]{1,2,0:T(8,128)(2,1)} copy(bf16[1,512,4096]{1,0,2:T(2,128)(2,1)} %bitcast.173) | data formatting | bytes 8388608
  287.4 6.5 %copy.33 = bf16[1,8,512,512]{3,2,1,0:T(8,128)(2,1)} copy(bf16[1,8,512,512]{2,3,1,0:T(8,128)(2,1)} %bitcast.179) | data formatting | bytes 8388608 | tf_op jit(solution)/shard_map/all_to_all | solution.py:74
  293.9 3.9 multiply_bitcast_fusion
  297.8 9.0 %gather_fusion.6 = bf16[96,128,512]{2,1,0:T(8,128)(2,1)} fusion(bf16[32,128,512]{2,1,0:T(8,128)(2,1)} %multiply_bitcast_fusion, s32[1024]{0:T(1024)S(1)} %pad_clamp_fusion.3), kind=kCustom, calls=%fused_computation.6 | custom fusion | bytes 25166208 | tf_op jit(solution)/shard_map/gather | solution.py:42
  306.8 9.0 %gather_fusion.7 = bf16[96,128,512]{2,1,0:T(8,128)(2,1)} fusion(bf16[32,128,512]{2,1,0:T(8,128)(2,1)} %multiply_bitcast_fusion, s32[1024]{0:T(1024)S(1)} %pad_clamp_fusion.2), kind=kCustom, calls=%fused_computation.7 | custom fusion | bytes 25166208 | tf_op jit(solution)/shard_map/gather | solution.py:42
  315.8 5.9 %fusion.4 = bf16[1,8,128,512]{3,2,1,0:T(8,128)(2,1)S(1)} fusion(bf16[8,12,128,512]{3,2,1,0:T(8,128)(2,1)} %bitcast.168, bf16[12,128,128]{2,1,0:T(8,128)(2,1)S(1)} %gather_fusion), kind=kOutput, calls=%fused_computation.28 | convolution fusion | flops 1611137024 | bytes 14024704 | tf_op jit(solution)/shard_map/pjkcn,krc->pjrn/dot_general | solution.py:44
  321.7 2.3 copy-done.2
  324.0 3.0 fusion.5
  327.0 9.0 %gather_fusion.8 = bf16[96,128,512]{2,1,0:T(8,128)(2,1)} fusion(bf16[32,128,512]{2,1,0:T(8,128)(2,1)} %multiply_bitcast_fusion, s32[1024]{0:T(1024)S(1)} %pad_clamp_fusion.1), kind=kCustom, calls=%fused_computation.8 | custom fusion | bytes 25166208 | tf_op jit(solution)/shard_map/gather | solution.py:42
  336.0 6.7 %fusion.6 = bf16[1,8,128,512]{3,2,1,0:T(8,128)(2,1)} fusion(bf16[8,12,128,512]{3,2,1,0:T(8,128)(2,1)} %bitcast.171, bf16[12,128,128]{2,1,0:T(8,128)(2,1)S(1)} %gather_fusion), kind=kOutput, calls=%fused_computation.30 | convolution fusion | flops 1611137024 | bytes 14024704 | tf_op jit(solution)/shard_map/pjkcn,krc->pjrn/dot_general | solution.py:44
  342.6 9.0 %gather_fusion.9 = bf16[96,128,512]{2,1,0:T(8,128)(2,1)} fusion(bf16[32,128,512]{2,1,0:T(8,128)(2,1)} %multiply_bitcast_fusion, s32[1024]{0:T(1024)S(1)} %pad_clamp_fusion), kind=kCustom, calls=%fused_computation.9 | custom fusion | bytes 25166208 | tf_op jit(solution)/shard_map/gather | solution.py:42
  351.7 5.9 %fusion.7 = bf16[1,8,128,512]{3,2,1,0:T(8,128)(2,1)S(1)} fusion(bf16[8,12,128,512]{3,2,1,0:T(8,128)(2,1)} %bitcast.170, bf16[12,128,128]{2,1,0:T(8,128)(2,1)S(1)} %gather_fusion), kind=kOutput, calls=%fused_computation.31 | convolution fusion | flops 1611137024 | bytes 14024704 | tf_op jit(solution)/shard_map/pjkcn,krc->pjrn/dot_general | solution.py:44
  357.6 0.6 pad_maximum_fusion.1
  358.1 0.0 copy-start.1
  358.2 5.1 %select_convert_fusion = bf16[2,4096,512]{2,1,0:T(8,128)(2,1)} fusion(bf16[4096,512]{1,0:T(8,128)(2,1)S(1)} %bitcast.182, pred[2]{0:T(512)(128)(4,1)S(1)} %iota_compare_fusion), kind=kLoop, calls=%fused_computation.10 | loop fusion | flops 4194304 | bytes 12582914 | tf_op jit(solution)/shard_map/convert_element_type | solution.py:84
  363.2 0.0 reduce-scatter.2.cloned.1.call-update
  363.3 70.7 %reduce-scatter.2.cloned.1.call-done = bf16[2,1024,512]{2,1,0:T(8,128)(2,1)} async-done(((bf16[2,4096,512]{2,1,0:T(8,128)(2,1)}), bf16[2,1024,512]{2,1,0:T(8,128)(2,1)}) %reduce-scatter.2.cloned.1.call-update) | async-done | bytes 2097168 | tf_op jit(solution)/shard_map/reduce_scatter | solution.py:83
  433.9 4.2 convert_element_type.112
  (38 shorter events, 0.2 us)
Async XLA Ops:
  6.5 40.3 %copy-start = (bf16[16,128,128]{2,1,0:T(8,128)(2,1)S(1)}, bf16[16,128,128]{2,1,0:T(8,128)(2,1)}, u32[]{:S(2)}) copy-start(bf16[16,128,128]{2,1,0:T(8,128)(2,1)} %param.16) | copy-start | bytes 1572868
  6.5 11.2 %copy-start.10 = (s32[2,4096]{1,0:T(2,128)S(1)}, s32[2,4096]{1,0:T(2,128)}, u32[]{:S(2)}) copy-start(s32[2,4096]{1,0:T(2,128)} %param.15) | copy-start | bytes 98308
  6.5 11.2 %copy-start.11 = (s32[2,4096]{1,0:T(2,128)S(1)}, s32[2,4096]{1,0:T(2,128)}, u32[]{:S(2)}) copy-start(s32[2,4096]{1,0:T(2,128)} %param.12) | copy-start | bytes 98308
  17.9 10.4 %copy-start.8 = (s32[2,32,12]{1,0,2:T(2,128)S(1)}, s32[2,32,12]{1,0,2:T(2,128)}, u32[]{:S(2)}) copy-start(s32[2,32,12]{1,0,2:T(2,128)} %param.10) | copy-start | bytes 9220
  17.9 10.8 %copy-start.12 = (s32[2,12]{1,0:T(2,128)S(1)}, s32[2,12]{1,0:T(2,128)}, u32[]{:S(2)}) copy-start(s32[2,12]{1,0:T(2,128)} %param.14) | copy-start | bytes 292
  17.9 10.8 %copy-start.13 = (s32[2,12]{1,0:T(2,128)S(1)}, s32[2,12]{1,0:T(2,128)}, u32[]{:S(2)}) copy-start(s32[2,12]{1,0:T(2,128)} %param.11) | copy-start | bytes 292
  47.4 8.9 %copy-start.3 = (bf16[96,512,128]{2,1,0:T(8,128)(2,1)S(1)}, bf16[96,512,128]{2,1,0:T(8,128)(2,1)}, u32[]{:S(2)}) copy-start(bf16[96,512,128]{2,1,0:T(8,128)(2,1)} %gather_fusion.3) | copy-start | bytes 37748740
  88.6 8.8 %copy-start.6 = (bf16[1,512,8,128]{1,3,2,0:T(8,128)(2,1)S(1)}, bf16[1,512,8,128]{1,3,2,0:T(8,128)(2,1)}, u32[]{:S(2)}) copy-start(bf16[1,512,8,128]{1,3,2,0:T(8,128)(2,1)} %fusion.2) | copy-start | bytes 3145732
  163.5 15.2 %copy-start.9 = (s32[2,32,12]{1,0,2:T(2,128)S(1)}, s32[2,32,12]{1,0,2:T(2,128)}, u32[]{:S(2)}) copy-start(s32[2,32,12]{1,0,2:T(2,128)} %param.13) | copy-start | bytes 9220
  163.5 16.0 %copy-start.7 = (bf16[16,128,128]{2,1,0:T(8,128)(2,1)S(1)}, bf16[16,128,128]{2,1,0:T(8,128)(2,1)}, u32[]{:S(2)}) copy-start(bf16[16,128,128]{2,1,0:T(8,128)(2,1)} %param.17) | copy-start | bytes 1572868
  171.4 100.6 %all-to-all-start = ((bf16[8,2,131072]{2,1,0:T(2,128)(2,1)}), bf16[8,2,131072]{2,1,0:T(2,128)(2,1)}, u32[]{:S(2)}, u32[]{:S(2)}) async-start(bf16[8,2,131072]{2,1,0:T(2,128)(2,1)} %reshape.535), calls=%async_computation | async-start | bytes 8388608 | tf_op jit(solution)/shard_map/all_to_all | solution.py:74
  178.7 255.2 %reduce-scatter.2.cloned.1.call-start = ((), (), s32[]{:S(2)}) async-start(), calls=%async_computation.2 | async-start | bytes 10485760 | tf_op jit(solution)/shard_map/reduce_scatter | solution.py:83
  315.8 8.2 %copy-start.2 = (bf16[96,128,512]{2,1,0:T(8,128)(2,1)S(1)}, bf16[96,128,512]{2,1,0:T(8,128)(2,1)}, u32[]{:S(2)}) copy-start(bf16[96,128,512]{2,1,0:T(8,128)(2,1)} %gather_fusion.7) | copy-start | bytes 37748740
  351.7 5.9 %copy-start.4 = (bf16[1,8,128,512]{3,2,1,0:T(8,128)(2,1)S(1)}, bf16[1,8,128,512]{3,2,1,0:T(8,128)(2,1)}, u32[]{:S(2)}) copy-start(bf16[1,8,128,512]{3,2,1,0:T(8,128)(2,1)} %fusion.5) | copy-start | bytes 3145732
  351.7 5.9 %copy-start.5 = (bf16[1,8,128,512]{3,2,1,0:T(8,128)(2,1)S(1)}, bf16[1,8,128,512]{3,2,1,0:T(8,128)(2,1)}, u32[]{:S(2)}) copy-start(bf16[1,8,128,512]{3,2,1,0:T(8,128)(2,1)} %fusion.6) | copy-start | bytes 3145732
  358.1 80.0 %copy-start.1 = (bf16[16,128,128]{2,1,0:T(8,128)(2,1)S(1)}, bf16[16,128,128]{2,1,0:T(8,128)(2,1)}, u32[]{:S(2)}) copy-start(bf16[16,128,128]{2,1,0:T(8,128)(2,1)} %param.16) | copy-start | bytes 1572868
Sparse Core Ops, SparseCore 0:
  363.4 70.5 reduce-scatter.1
where the time goes:
time: 446 us; the launch traced here: 445 us
  local copies, waits for them, and re-layouts  162 us (36%)
  waiting for transfers between devices  162 us (36%)
  matrix products  52.9 us (12%)
  other arithmetic  47.1 us (11%)
  between operations  13.7 us (3%)
  starting transfers between devices  7.33 us (2%)
    all_to_all x1, waiting for transfers between devices, local(): lax.all_to_all(half, 'str', split_axis=2, concat_axis=1, tiled=True)  91.7 us
    reduce_scatter x1, waiting for transfers between devices, local(): lax.psum_scatter(padded.astype(jnp.bfloat16), 'fac', scatter_dimension=1,...  70.7 us
    reshape x1, local copies, waits for them, and re-layouts, apply_beta(): jnp.concatenate(pieces, axis=2).reshape(part_count, height, column_count)  36.5 us
    gather x4, local copies, waits for them, and re-layouts, apply_beta(): gathered = blocks[:, :, chosen]  36.1 us
    gather x4, local copies, waits for them, and re-layouts, apply_alpha(): gathered = blocks[:, chosen]  36 us
    unnamed x41, local copies, waits for them, and re-layouts  33.3 us
    dot_general x4, matrix products, apply_beta(): jnp.einsum('pajkc,krc->pajr', gathered, weights, preferred_element_type=j...  31.5 us
    unnamed x1, other arithmetic  28.5 us
  transfers between devices with their start and end apart: 2, of which 2 were waited for; matrix products, arithmetic and copies ran while one was open for 0% of the time, Pallas kernels for 0%

commit v1 on v0

--- a/solution.py
+++ b/solution.py
@@ -71,7 +71,10 @@
     alpha_kinds = lax.dynamic_index_in_dim(alpha_tile, factor, 0, keepdims=False)
     alpha_signs = lax.dynamic_index_in_dim(alpha_flip, factor, 0, keepdims=False)
     mixed = apply_alpha(
-        lax.all_to_all(half, "str", split_axis=2, concat_axis=1, tiled=True),
+        jnp.concatenate(
+            lax.all_to_all(jnp.stack(jnp.split(half, lax.axis_size("str"), axis=2)), "str", 0, 0),
+            axis=1,
+        ),
         alpha_ids,
         alpha_kinds,
         alpha_signs,

time: 446 us -> 368 us (0.83)
  local copies, waits for them, and re-layouts: 162 us -> 112 us
  other arithmetic: 47.1 us -> 18.6 us
    reshape x1 -> x0, local copies, waits for them, and re-layouts: 36.5 us -> none  [apply_beta(): jnp.concatenate(pieces, axis=2).reshape(part_count, height, column_count)]
    unnamed x1 -> x0, other arithmetic: 28.5 us -> none
    unnamed x41 -> x52, local copies, waits for them, and re-layouts: 33.3 us -> 24.6 us
    all_to_all x1 -> x0, local copies, waits for them, and re-layouts: 6.46 us -> none  [local(): lax.all_to_all(half, 'str', split_axis=2, concat_axis=1, tiled=True)]
where the time goes in v1:
time: 368 us; the launch traced here: 367 us
  waiting for transfers between devices  162 us (44%)
  local copies, waits for them, and re-layouts  112 us (30%)
  matrix products  52.9 us (14%)
  other arithmetic  18.6 us (5%)
  between operations  13.7 us (4%)
  starting transfers between devices  7.45 us (2%)
    all_to_all x1, waiting for transfers between devices, local(): lax.all_to_all(jnp.stack(jnp.split(half, lax.axis_size('str'), axis=2)),...  91.7 us
    reduce_scatter x1, waiting for transfers between devices, local(): lax.psum_scatter(padded.astype(jnp.bfloat16), 'fac', scatter_dimension=1,...  70.7 us
    gather x4, local copies, waits for them, and re-layouts, apply_beta(): gathered = blocks[:, :, chosen]  36.1 us
    gather x4, local copies, waits for them, and re-layouts, apply_alpha(): gathered = blocks[:, chosen]  36.1 us
    dot_general x4, matrix products, apply_beta(): jnp.einsum('pajkc,krc->pajr', gathered, weights, preferred_element_type=j...  31.6 us
    unnamed x52, local copies, waits for them, and re-layouts  24.6 us
    dot_general x4, matrix products, apply_alpha(): jnp.einsum('pjkcn,krc->pjrn', gathered, weights, preferred_element_type=j...  21.4 us
    all_to_all x1, starting transfers between devices, local(): lax.all_to_all(jnp.stack(jnp.split(half, lax.axis_size('str'), axis=2)),...  7.41 us
  transfers between devices with their start and end apart: 2, of which 2 were waited for; matrix products, arithmetic and copies ran while one was open for 0% of the time, Pallas kernels for 0%

profile of v1, /device:TPU:0, one launch (start us, length us, event | category | flops | bytes accessed | tf_op | source)
XLA Modules:
  0.0 367.3 jit_solution(14059652385584747454)
XLA Ops:
  6.5 4.8 %constant_dynamic-slice_fusion.9 = bf16[1,512,4096]{2,1,0:T(8,128)(2,1)} fusion(bf16[2,512,4096]{2,1,0:T(8,128)(2,1)} %param.9, s32[]{:T(128)S(6)} %select_n.134), kind=kLoop, calls=%fused_computation.77 | loop fusion | bytes 8388612 | tf_op jit(solution)/shard_map/jit(dynamic_index_in_dim)/dynamic_slice | solution.py:65
  11.3 6.5 %copy.64 = bf16[1,512,4096]{1,2,0:T(8,128)(2,1)} copy(bf16[1,512,4096]{2,1,0:T(8,128)(2,1)} %constant_dynamic-slice_fusion.9) | data formatting | bytes 8388608
  17.8 3.9 %broadcast_multiply_fusion = bf16[1,512,4096]{1,2,0:T(8,128)(2,1)} fusion(bf16[1,512,4096]{1,2,0:T(8,128)(2,1)} %copy.64, bf16[4096]{0:T(1024)(128)(2,1)S(1)} %convert_reduce_fusion.1), kind=kLoop, calls=%fused_computation.23 | loop fusion | flops 2097152 | bytes 8396800 | tf_op jit(solution)/shard_map/mul | solution.py:12
  21.8 6.5 %copy.43 = bf16[512,32,128]{2,0,1:T(8,128)(2,1)} copy(bf16[512,32,128]{0,2,1:T(8,128)(2,1)} %bitcast.185) | data formatting | bytes 8388608 | tf_op jit(solution)/shard_map/reshape | solution.py:13
  28.3 0.1 constant_dynamic-slice_fusion.5
  28.4 0.1 copy.66
  28.5 0.1 copy.67
  28.5 0.1 reshape.419
  28.7 0.1 reshape.437
  28.8 9.0 %gather_fusion.1 = bf16[96,512,128]{2,1,0:T(8,128)(2,1)} fusion(bf16[512,32,128]{2,0,1:T(8,128)(2,1)} %copy.43, s32[1024]{0:T(1024)S(1)} %pad_clamp_fusion.8), kind=kCustom, calls=%fused_computation.1 | custom fusion | bytes 25166208 | tf_op jit(solution)/shard_map/gather | solution.py:20
  37.8 9.0 %gather_fusion.3 = bf16[96,512,128]{2,1,0:T(8,128)(2,1)} fusion(bf16[512,32,128]{2,0,1:T(8,128)(2,1)} %copy.43, s32[1024]{0:T(1024)S(1)} %pad_clamp_fusion.6), kind=kCustom, calls=%fused_computation.3 | custom fusion | bytes 25166208 | tf_op jit(solution)/shard_map/gather | solution.py:20
  46.8 0.6 gather_fusion.2
  47.4 8.9 %fusion = bf16[1,512,8,128]{1,3,2,0:T(8,128)(2,1)S(1)} fusion(bf16[512,8,12,128]{3,0,2,1:T(8,128)(2,1)} %bitcast.181, bf16[12,128,128]{2,1,0:T(8,128)(2,1)S(1)} %gather_fusion.2), kind=kOutput, calls=%fused_computation.24 | convolution fusion | flops 1611137024 | bytes 14024704 | tf_op jit(solution)/shard_map/pajkc,krc->pajr/dot_general | solution.py:22
  56.3 4.2 %fusion.1 = bf16[1,512,8,128]{1,3,2,0:T(8,128)(2,1)S(1)} fusion(bf16[512,8,12,128]{3,0,2,1:T(8,128)(2,1)S(1)} %bitcast.182, bf16[12,128,128]{2,1,0:T(8,128)(2,1)S(1)} %gather_fusion.2), kind=kOutput, calls=%fused_computation.25 | convolution fusion | flops 1611137024 | bytes 14024704 | tf_op jit(solution)/shard_map/pajkc,krc->pajr/dot_general | solution.py:22
  60.5 0.1 copy.68
  60.6 0.1 copy.69
  60.7 0.1 reshape.447
  60.8 9.0 %gather_fusion.4 = bf16[96,512,128]{2,1,0:T(8,128)(2,1)} fusion(bf16[512,32,128]{2,0,1:T(8,128)(2,1)} %copy.43, s32[1024]{0:T(1024)S(1)} %pad_clamp_fusion.5), kind=kCustom, calls=%fused_computation.4 | custom fusion | bytes 25166208 | tf_op jit(solution)/shard_map/gather | solution.py:20
  69.8 9.7 %fusion.2 = bf16[1,512,8,128]{1,3,2,0:T(8,128)(2,1)} fusion(bf16[512,8,12,128]{3,0,2,1:T(8,128)(2,1)} %bitcast.184, bf16[12,128,128]{2,1,0:T(8,128)(2,1)S(1)} %gather_fusion.2), kind=kOutput, calls=%fused_computation.26 | convolution fusion | flops 1611137024 | bytes 14024704 | tf_op jit(solution)/shard_map/pajkc,krc->pajr/dot_general | solution.py:22
  79.5 0.1 reshape.457
  79.6 9.0 %gather_fusion.5 = bf16[96,512,128]{2,1,0:T(8,128)(2,1)} fusion(bf16[512,32,128]{2,0,1:T(8,128)(2,1)} %copy.43, s32[1024]{0:T(1024)S(1)} %pad_clamp_fusion.4), kind=kCustom, calls=%fused_computation.5 | custom fusion | bytes 25166208 | tf_op jit(solution)/shard_map/gather | solution.py:20
  88.6 8.8 %fusion.3 = bf16[1,512,8,128]{1,3,2,0:T(8,128)(2,1)S(1)} fusion(bf16[512,8,12,128]{3,0,2,1:T(8,128)(2,1)} %bitcast.183, bf16[12,128,128]{2,1,0:T(8,128)(2,1)S(1)} %gather_fusion.2), kind=kOutput, calls=%fused_computation.27 | convolution fusion | flops 1611137024 | bytes 14024704 | tf_op jit(solution)/shard_map/pajkc,krc->pajr/dot_general | solution.py:22
  97.5 0.6 pad_maximum_fusion
  98.0 1.4 fusion.20
  99.5 2.1 copy.70
  101.5 1.9 bitcast_dynamic-update-slice_fusion.7
  103.4 2.1 copy.71
  105.5 1.0 copy.72
  106.5 0.2 copy.73
  106.7 0.2 copy.74
  106.9 0.2 copy.75
  107.1 0.2 copy.76
  107.3 0.2 copy.77
  107.6 1.9 bitcast_dynamic-update-slice_fusion.6
  109.4 1.9 bitcast_dynamic-update-slice_fusion.5
  111.3 0.8 bitcast_dynamic-update-slice_fusion.4
  112.1 0.8 bitcast_dynamic-update-slice_fusion.3
  113.0 0.8 bitcast_dynamic-update-slice_fusion.2
  113.8 0.8 bitcast_dynamic-update-slice_fusion.1
  114.6 0.8 bitcast_dynamic-update-slice_fusion
  115.4 7.4 %all-to-all-start = ((bf16[8,1,512,512]{3,2,1,0:T(8,128)(2,1)}), bf16[8,1,512,512]{3,2,1,0:T(8,128)(2,1)}, u32[]{:S(2)}, u32[]{:S(2)}) async-start(bf16[8,1,512,512]{3,2,1,0:T(8,128)(2,1)} %bitcast_dynamic-update-slice_fusion), calls=%async_computation | async-start | bytes 8388608 | tf_op jit(solution)/shard_map/all_to_all | solution.py:75
  122.9 0.1 constant_dynamic-slice_fusion.2
  123.0 0.1 copy.79
  123.1 0.1 copy.80
  123.2 0.1 reshape.467
  123.3 0.1 reshape.477
  123.5 0.1 reshape.487
  123.6 0.1 reshape.497
  123.7 0.6 gather_fusion
  124.5 91.7 %all-to-all-done = bf16[8,1,512,512]{3,2,1,0:T(8,128)(2,1)} async-done(((bf16[8,1,512,512]{3,2,1,0:T(8,128)(2,1)}), bf16[8,1,512,512]{3,2,1,0:T(8,128)(2,1)}, u32[]{:S(2)}, u32[]{:S(2)}) %all-to-all-start) | async-done | bytes 4194336 | tf_op jit(solution)/shard_map/all_to_all | solution.py:75
  216.1 3.9 %multiply_bitcast_fusion = bf16[32,128,512]{2,1,0:T(8,128)(2,1)} fusion(bf16[1,32,128,512]{3,2,1,0:T(8,128)(2,1)} %bitcast.40, bf16[32,128]{1,0:T(8,128)(2,1)S(1)} %bitcast.188), kind=kLoop, calls=%fused_computation.14 | loop fusion | flops 2097152 | bytes 8396800 | tf_op jit(solution)/shard_map/mul | solution.py:34
  220.1 9.0 %gather_fusion.6 = bf16[96,128,512]{2,1,0:T(8,128)(2,1)} fusion(bf16[32,128,512]{2,1,0:T(8,128)(2,1)} %multiply_bitcast_fusion, s32[1024]{0:T(1024)S(1)} %pad_clamp_fusion.3), kind=kCustom, calls=%fused_computation.6 | custom fusion | bytes 25166208 | tf_op jit(solution)/shard_map/gather | solution.py:42
  229.1 9.0 %gather_fusion.7 = bf16[96,128,512]{2,1,0:T(8,128)(2,1)} fusion(bf16[32,128,512]{2,1,0:T(8,128)(2,1)} %multiply_bitcast_fusion, s32[1024]{0:T(1024)S(1)} %pad_clamp_fusion.2), kind=kCustom, calls=%fused_computation.7 | custom fusion | bytes 25166208 | tf_op jit(solution)/shard_map/gather | solution.py:42
  238.1 5.9 %fusion.4 = bf16[1,8,128,512]{3,2,1,0:T(8,128)(2,1)S(1)} fusion(bf16[8,12,128,512]{3,2,1,0:T(8,128)(2,1)} %bitcast.177, bf16[12,128,128]{2,1,0:T(8,128)(2,1)S(1)} %gather_fusion), kind=kOutput, calls=%fused_computation.28 | convolution fusion | flops 1611137024 | bytes 14024704 | tf_op jit(solution)/shard_map/pjkcn,krc->pjrn/dot_general | solution.py:44
  244.0 2.3 copy-done.2
  246.3 3.0 fusion.5
  249.3 9.0 %gather_fusion.8 = bf16[96,128,512]{2,1,0:T(8,128)(2,1)} fusion(bf16[32,128,512]{2,1,0:T(8,128)(2,1)} %multiply_bitcast_fusion, s32[1024]{0:T(1024)S(1)} %pad_clamp_fusion.1), kind=kCustom, calls=%fused_computation.8 | custom fusion | bytes 25166208 | tf_op jit(solution)/shard_map/gather | solution.py:42
  258.3 6.7 %fusion.6 = bf16[1,8,128,512]{3,2,1,0:T(8,128)(2,1)} fusion(bf16[8,12,128,512]{3,2,1,0:T(8,128)(2,1)} %bitcast.180, bf16[12,128,128]{2,1,0:T(8,128)(2,1)S(1)} %gather_fusion), kind=kOutput, calls=%fused_computation.30 | convolution fusion | flops 1611137024 | bytes 14024704 | tf_op jit(solution)/shard_map/pjkcn,krc->pjrn/dot_general | solution.py:44
  264.9 9.0 %gather_fusion.9 = bf16[96,128,512]{2,1,0:T(8,128)(2,1)} fusion(bf16[32,128,512]{2,1,0:T(8,128)(2,1)} %multiply_bitcast_fusion, s32[1024]{0:T(1024)S(1)} %pad_clamp_fusion), kind=kCustom, calls=%fused_computation.9 | custom fusion | bytes 25166208 | tf_op jit(solution)/shard_map/gather | solution.py:42
  274.0 5.9 %fusion.7 = bf16[1,8,128,512]{3,2,1,0:T(8,128)(2,1)S(1)} fusion(bf16[8,12,128,512]{3,2,1,0:T(8,128)(2,1)} %bitcast.179, bf16[12,128,128]{2,1,0:T(8,128)(2,1)S(1)} %gather_fusion), kind=kOutput, calls=%fused_computation.31 | convolution fusion | flops 1611137024 | bytes 14024704 | tf_op jit(solution)/shard_map/pjkcn,krc->pjrn/dot_general | solution.py:44
  279.9 0.6 pad_maximum_fusion.1
  280.4 5.1 %select_convert_fusion = bf16[2,4096,512]{2,1,0:T(8,128)(2,1)} fusion(bf16[4096,512]{1,0:T(8,128)(2,1)S(1)} %bitcast.187, pred[2]{0:T(512)(128)(4,1)S(1)} %iota_compare_fusion), kind=kLoop, calls=%fused_computation.10 | loop fusion | flops 4194304 | bytes 12582914 | tf_op jit(solution)/shard_map/convert_element_type | solution.py:87
  285.6 70.7 %reduce-scatter.2.cloned.1.call-done = bf16[2,1024,512]{2,1,0:T(8,128)(2,1)} async-done(((bf16[2,4096,512]{2,1,0:T(8,128)(2,1)}), bf16[2,1024,512]{2,1,0:T(8,128)(2,1)}) %reduce-scatter.2.cloned.1.call-update) | async-done | bytes 2097168 | tf_op jit(solution)/shard_map/reduce_scatter | solution.py:86
  356.3 4.2 %convert_element_type.112 = f32[2,1024,512]{2,1,0:T(8,128)} convert(bf16[2,1024,512]{2,1,0:T(8,128)(2,1)} %reduce-scatter.2.cloned.1.call-done) | non-fusion elementwise | flops 1048576 | bytes 6291456 | tf_op jit(solution)/shard_map/convert_element_type | solution.py:88
  (49 shorter events, 0.5 us)
Async XLA Ops:
  6.5 40.3 %copy-start = (bf16[16,128,128]{2,1,0:T(8,128)(2,1)S(1)}, bf16[16,128,128]{2,1,0:T(8,128)(2,1)}, u32[]{:S(2)}) copy-start(bf16[16,128,128]{2,1,0:T(8,128)(2,1)} %param.16) | copy-start | bytes 1572868
  11.3 6.5 %copy-start.10 = (s32[2,4096]{1,0:T(2,128)S(1)}, s32[2,4096]{1,0:T(2,128)}, u32[]{:S(2)}) copy-start(s32[2,4096]{1,0:T(2,128)} %param.12) | copy-start | bytes 98308
  21.8 6.5 %copy-start.8 = (s32[2,32,12]{1,0,2:T(2,128)S(1)}, s32[2,32,12]{1,0,2:T(2,128)}, u32[]{:S(2)}) copy-start(s32[2,32,12]{1,0,2:T(2,128)} %param.10) | copy-start | bytes 9220
  21.8 6.9 %copy-start.12 = (s32[2,12]{1,0:T(2,128)S(1)}, s32[2,12]{1,0:T(2,128)}, u32[]{:S(2)}) copy-start(s32[2,12]{1,0:T(2,128)} %param.14) | copy-start | bytes 292
  21.8 6.9 %copy-start.13 = (s32[2,12]{1,0:T(2,128)S(1)}, s32[2,12]{1,0:T(2,128)}, u32[]{:S(2)}) copy-start(s32[2,12]{1,0:T(2,128)} %param.11) | copy-start | bytes 292
  47.4 8.9 %copy-start.3 = (bf16[96,512,128]{2,1,0:T(8,128)(2,1)S(1)}, bf16[96,512,128]{2,1,0:T(8,128)(2,1)}, u32[]{:S(2)}) copy-start(bf16[96,512,128]{2,1,0:T(8,128)(2,1)} %gather_fusion.3) | copy-start | bytes 37748740
  88.6 8.8 %copy-start.6 = (bf16[1,512,8,128]{1,3,2,0:T(8,128)(2,1)S(1)}, bf16[1,512,8,128]{1,3,2,0:T(8,128)(2,1)}, u32[]{:S(2)}) copy-start(bf16[1,512,8,128]{1,3,2,0:T(8,128)(2,1)} %fusion.2) | copy-start | bytes 3145732
  115.4 7.5 %copy-start.9 = (s32[2,32,12]{1,0,2:T(2,128)S(1)}, s32[2,32,12]{1,0,2:T(2,128)}, u32[]{:S(2)}) copy-start(s32[2,32,12]{1,0,2:T(2,128)} %param.13) | copy-start | bytes 9220
  115.4 8.3 %copy-start.7 = (bf16[16,128,128]{2,1,0:T(8,128)(2,1)S(1)}, bf16[16,128,128]{2,1,0:T(8,128)(2,1)}, u32[]{:S(2)}) copy-start(bf16[16,128,128]{2,1,0:T(8,128)(2,1)} %param.17) | copy-start | bytes 1572868
  115.4 8.9 %copy-start.11 = (s32[2,4096]{1,0:T(2,128)S(1)}, s32[2,4096]{1,0:T(2,128)}, u32[]{:S(2)}) copy-start(s32[2,4096]{1,0:T(2,128)} %param.15) | copy-start | bytes 98308
  115.4 100.7 %all-to-all-start = ((bf16[8,1,512,512]{3,2,1,0:T(8,128)(2,1)}), bf16[8,1,512,512]{3,2,1,0:T(8,128)(2,1)}, u32[]{:S(2)}, u32[]{:S(2)}) async-start(bf16[8,1,512,512]{3,2,1,0:T(8,128)(2,1)} %bitcast_dynamic-update-slice_fusion), calls=%async_computation | async-start | bytes 8388608 | tf_op jit(solution)/shard_map/all_to_all | solution.py:75
  122.9 233.4 %reduce-scatter.2.cloned.1.call-start = ((), (), s32[]{:S(2)}) async-start(), calls=%async_computation.2 | async-start | bytes 10485760 | tf_op jit(solution)/shard_map/reduce_scatter | solution.py:86
  238.1 8.2 %copy-start.2 = (bf16[96,128,512]{2,1,0:T(8,128)(2,1)S(1)}, bf16[96,128,512]{2,1,0:T(8,128)(2,1)}, u32[]{:S(2)}) copy-start(bf16[96,128,512]{2,1,0:T(8,128)(2,1)} %gather_fusion.7) | copy-start | bytes 37748740
  274.0 5.9 %copy-start.4 = (bf16[1,8,128,512]{3,2,1,0:T(8,128)(2,1)S(1)}, bf16[1,8,128,512]{3,2,1,0:T(8,128)(2,1)}, u32[]{:S(2)}) copy-start(bf16[1,8,128,512]{3,2,1,0:T(8,128)(2,1)} %fusion.5) | copy-start | bytes 3145732
  274.0 5.9 %copy-start.5 = (bf16[1,8,128,512]{3,2,1,0:T(8,128)(2,1)S(1)}, bf16[1,8,128,512]{3,2,1,0:T(8,128)(2,1)}, u32[]{:S(2)}) copy-start(bf16[1,8,128,512]{3,2,1,0:T(8,128)(2,1)} %fusion.6) | copy-start | bytes 3145732
  285.6 74.9 %copy-start.1 = (bf16[16,128,128]{2,1,0:T(8,128)(2,1)S(1)}, bf16[16,128,128]{2,1,0:T(8,128)(2,1)}, u32[]{:S(2)}) copy-start(bf16[16,128,128]{2,1,0:T(8,128)(2,1)} %param.16) | copy-start | bytes 1572868
Sparse Core Ops, SparseCore 0:
  285.7 70.5 reduce-scatter.1
